TPU v7x, 128 devices: a whole 4x4x4 slice. The times are simulated.
128 devices in a mesh: rows: 32 (over z, x, core), rep: 4 (over y).
Axes of the slice: x: 4, y: 4, z: 4, core: 2. Of those that a mesh axis runs over, the one named last changes fastest.
Arguments:
- features: bfloat16 [65536, 512], P(('rows', 'rep')), may hold values from -6 to 6
- weight: bfloat16 [512, 512], replicated, may hold values from -6 to 6
- out_bias: float32 [512], replicated, may hold values from -4 to 4
- degree: int32 [65536], P(('rows', 'rep')), may hold values from 256 to 1023
- tile_row: int32 [8192], P(('rows', 'rep')), may hold values from 0 to 15, as said below
- tile_col: int32 [8192], P(('rows', 'rep')), may hold values from 0 to 127, as said below
- tile_value: bfloat16 [8192, 128, 128], P(('rows', 'rep')), may hold values from 0 to 3, as said below
- cotangent: bfloat16 [65536, 512], P(('rows', 'rep')), may hold values from -6 to 6
Outputs:
- hidden_out: bfloat16 [65536, 512], P(('rows', 'rep'))
- grad_input: bfloat16 [65536, 512], P(('rows', 'rep'))
- grad_weight: float32 [512, 512], replicated
Inputs may be any that keep to these rules, and one draw needn't show every extreme that they name: `tile_row`: on each device the slots that hold edges come first; every later slot has an all-zero tile and both of its indices 0. Every node block's diagonal block is among its device's slots. Columns of a device's group are numbered slab by slab: tile_col = j * 4 + b names node block (j * 4 + c) * 4 + b. `tile_value`: all slots together form a symmetric adjacency: for every slot with tile V on global blocks (g, h) there is a slot on (h, g) with tile V transposed, and a diagonal block's tile is symmetric. Entries are 0 or between 0.1 and 3.
All inputs are finite; a program needn't handle non-finite values.
Results may differ from a plain program's by a relative error of at most 0.0061.
Values may be sent and summed in bfloat16 or wider, within the bound.
A program may use at most 128 MiB of HBM per device.

v0:
```python
import jax
import jax.numpy as jnp
from jax import lax
from jax.sharding import PartitionSpec as P


def aggregate_slots(panels, group_rows_all, group_cols_all, tiles_all, out_blocks):
    tile_size = tiles_all.shape[1]
    feat_width = panels.shape[1]
    panel_blocks = panels.reshape(-1, tile_size, feat_width)
    group_count = tiles_all.shape[0] // 8

    def add_group(totals, bundle):
        group_rows, group_cols, group_tiles = bundle
        products = jnp.einsum(
            "sij,sjf->sif",
            group_tiles,
            panel_blocks[group_cols],
            preferred_element_type=jnp.float32,
        )
        return (totals.at[group_rows].add(products), None)

    initial = jnp.zeros((out_blocks, tile_size, feat_width), jnp.float32)
    bundles = (
        group_rows_all.reshape(group_count, 8),
        group_cols_all.reshape(group_count, 8),
        tiles_all.reshape(group_count, 8, tile_size, tile_size),
    )
    totals, _ = lax.scan(add_group, initial, bundles)
    return totals.reshape(out_blocks * tile_size, feat_width)


def shards(features, weight, out_bias, degree, tile_row, tile_col, tile_value, cotangent):
    tile_size = tile_value.shape[1]
    nodes_dev = features.shape[0]
    feat_width = features.shape[1]
    block_count = nodes_dev // tile_size
    rep_count = lax.axis_size("rep")
    row_scale = lax.rsqrt(degree.astype(jnp.float32))[:, None]
    scaled = (jnp.dot(features, weight, preferred_element_type=jnp.float32) * row_scale).astype(
        jnp.bfloat16
    )
    panels = lax.all_gather(scaled, "rows", axis=0, tiled=True)
    slab_part = aggregate_slots(panels, tile_row, tile_col, tile_value, rep_count * block_count)
    aggregate = lax.psum_scatter(slab_part, "rep", scatter_dimension=0, tiled=True) * row_scale
    pre_act = aggregate + out_bias
    hidden_out = jax.nn.silu(pre_act).astype(jnp.bfloat16)
    sigmoid_pre = jax.nn.sigmoid(pre_act)
    grad_pre = cotangent.astype(jnp.float32) * sigmoid_pre * (1.0 + pre_act * (1.0 - sigmoid_pre))
    scaled_grad = (grad_pre * row_scale).astype(jnp.bfloat16)
    slab_grads = lax.all_gather(scaled_grad, "rep", axis=0, tiled=True)
    grad_blocks = slab_grads.reshape(rep_count * block_count, tile_size, feat_width)
    products = jnp.einsum(
        "sji,sjf->sif", tile_value, grad_blocks[tile_row], preferred_element_type=jnp.float32
    )
    block_total = nodes_dev * lax.axis_size("rows") // tile_size
    target = jnp.where((tile_col >= 0) & (tile_col < block_total), tile_col, block_total)
    totals = jnp.zeros((block_total, tile_size, feat_width), jnp.float32)
    totals = totals.at[target].add(products, mode="drop")
    back_total = lax.psum_scatter(
        totals.reshape(nodes_dev * lax.axis_size("rows"), feat_width),
        "rows",
        scatter_dimension=0,
        tiled=True,
    )
    back_sum = (back_total * row_scale).astype(jnp.bfloat16)
    grad_input = lax.dot_general(
        back_sum, weight, (((1,), (1,)), ((), ())), preferred_element_type=jnp.float32
    ).astype(jnp.bfloat16)
    local_weight = lax.dot_general(
        features, back_sum, (((0,), (0,)), ((), ())), preferred_element_type=jnp.float32
    )
    grad_weight = lax.psum(local_weight, ("rows", "rep"))
    return (hidden_out, grad_input, grad_weight)


def solution(mesh):
    placed = (
        P(("rows", "rep"), None),
        P(),
        P(),
        P(("rows", "rep")),
        P(("rows", "rep")),
        P(("rows", "rep")),
        P(("rows", "rep"), None, None),
        P(("rows", "rep"), None),
    )
    return jax.shard_map(
        shards,
        mesh=mesh,
        in_specs=placed,
        out_specs=(P(("rows", "rep"), None), P(("rows", "rep"), None), P()),
        check_vma=False,
    )
```

profile of v0, /device:TPU:1, one launch (start us, length us, event | category | flops | bytes accessed | tf_op | source)
XLA Modules:
  0.0 688.1 jit_solution(9885065440772527485)
XLA Ops:
  12.0 75.1 %all-gather.3.cloned.1.call-done = bf16[16384,512]{1,0:T(8,128)(2,1)} async-done(((bf16[512,512]{1,0:T(8,128)(2,1)}), bf16[16384,512]{1,0:T(8,128)(2,1)}) %all-gather.3.cloned.1.call-update) | async-done | bytes 16777232 | tf_op jit(solution)/shard_map/all_gather | solution.py:43
  89.6 107.3 %while.10 = (s32[]{:T(128)}, f32[16,128,512]{2,1,0:T(8,128)}, s32[8,8]{1,0:T(8,128)S(1)}, bf16[8,8,128,128]{3,2,1,0:T(8,128)(2,1)}, s32[8,8]{1,0:T(8,128)S(1)}, /*index=5*/bf16[128,128,512]{2,1,0:T(8,128)(2,1)}, s32[]{:T(128)}) while((s32[]{:T(128)}, f32[16,128,512]{2,1,0:T(8,128)}, s32[8,8]{1,0:T(8,128)S(1)}, ...), condition=%wide.region_2.3_spmd, body=%wide.region_0.2_spmd.sunk | while | flops 134743088 | bytes 11800893 | solution.py:29
  89.6 7.4 %gather_fusion = bf16[8,128,512]{2,1,0:T(8,128)(2,1)} fusion(bf16[128,128,512]{2,1,0:T(8,128)(2,1)} %get-tuple-element.118, s32[1024]{0:T(1024)S(1)} %pad_clamp_fusion.3), kind=kCustom, calls=%fused_computation.clone.1 | custom fusion | bytes 2097184 | tf_op jit(solution)/shard_map/while/body/eval_jaxpr/gather | solution.py:18
  98.7 4.4 scatter_fusion
  103.1 7.4 %gather_fusion = bf16[8,128,512]{2,1,0:T(8,128)(2,1)} fusion(bf16[128,128,512]{2,1,0:T(8,128)(2,1)} %get-tuple-element.118, s32[1024]{0:T(1024)S(1)} %pad_clamp_fusion.3), kind=kCustom, calls=%fused_computation.clone.1 | custom fusion | bytes 2097184 | tf_op jit(solution)/shard_map/while/body/eval_jaxpr/gather | solution.py:18
  112.2 4.3 scatter_fusion
  116.5 7.4 %gather_fusion = bf16[8,128,512]{2,1,0:T(8,128)(2,1)} fusion(bf16[128,128,512]{2,1,0:T(8,128)(2,1)} %get-tuple-element.118, s32[1024]{0:T(1024)S(1)} %pad_clamp_fusion.3), kind=kCustom, calls=%fused_computation.clone.1 | custom fusion | bytes 2097184 | tf_op jit(solution)/shard_map/while/body/eval_jaxpr/gather | solution.py:18
  129.7 7.4 %gather_fusion = bf16[8,128,512]{2,1,0:T(8,128)(2,1)} fusion(bf16[128,128,512]{2,1,0:T(8,128)(2,1)} %get-tuple-element.118, s32[1024]{0:T(1024)S(1)} %pad_clamp_fusion.3), kind=kCustom, calls=%fused_computation.clone.1 | custom fusion | bytes 2097184 | tf_op jit(solution)/shard_map/while/body/eval_jaxpr/gather | solution.py:18
  142.9 7.4 %gather_fusion = bf16[8,128,512]{2,1,0:T(8,128)(2,1)} fusion(bf16[128,128,512]{2,1,0:T(8,128)(2,1)} %get-tuple-element.118, s32[1024]{0:T(1024)S(1)} %pad_clamp_fusion.3), kind=kCustom, calls=%fused_computation.clone.1 | custom fusion | bytes 2097184 | tf_op jit(solution)/shard_map/while/body/eval_jaxpr/gather | solution.py:18
  156.3 7.4 %gather_fusion = bf16[8,128,512]{2,1,0:T(8,128)(2,1)} fusion(bf16[128,128,512]{2,1,0:T(8,128)(2,1)} %get-tuple-element.118, s32[1024]{0:T(1024)S(1)} %pad_clamp_fusion.3), kind=kCustom, calls=%fused_computation.clone.1 | custom fusion | bytes 2097184 | tf_op jit(solution)/shard_map/while/body/eval_jaxpr/gather | solution.py:18
  165.3 4.5 scatter_fusion
  169.8 7.4 %gather_fusion = bf16[8,128,512]{2,1,0:T(8,128)(2,1)} fusion(bf16[128,128,512]{2,1,0:T(8,128)(2,1)} %get-tuple-element.118, s32[1024]{0:T(1024)S(1)} %pad_clamp_fusion.3), kind=kCustom, calls=%fused_computation.clone.1 | custom fusion | bytes 2097184 | tf_op jit(solution)/shard_map/while/body/eval_jaxpr/gather | solution.py:18
  178.9 4.5 scatter_fusion
  183.4 7.4 %gather_fusion = bf16[8,128,512]{2,1,0:T(8,128)(2,1)} fusion(bf16[128,128,512]{2,1,0:T(8,128)(2,1)} %get-tuple-element.118, s32[1024]{0:T(1024)S(1)} %pad_clamp_fusion.3), kind=kCustom, calls=%fused_computation.clone.1 | custom fusion | bytes 2097184 | tf_op jit(solution)/shard_map/while/body/eval_jaxpr/gather | solution.py:18
  192.5 4.5 scatter_fusion
  197.0 46.4 %reduce-scatter.3.cloned.1.call-done = f32[512,512]{1,0:T(8,128)} async-done(((f32[2048,512]{1,0:T(8,128)}), f32[512,512]{1,0:T(8,128)}) %reduce-scatter.3.cloned.1.call-update) | async-done | bytes 1048592 | tf_op jit(solution)/shard_map/reduce_scatter | solution.py:45
  246.4 30.4 %all-gather.5.cloned.1.call-done = bf16[2048,512]{1,0:T(8,128)(2,1)} async-done(((bf16[512,512]{1,0:T(8,128)(2,1)}), bf16[2048,512]{1,0:T(8,128)(2,1)}) %all-gather.5.cloned.1.call-update) | async-done | bytes 2097168 | tf_op jit(solution)/shard_map/all_gather | solution.py:51
  276.8 7.2 %gather_fusion.1 = bf16[64,128,512]{2,1,0:T(8,128)(2,1)} fusion(bf16[16,128,512]{2,1,0:T(8,128)(2,1)} %bitcast.45, s32[1024]{0:T(1024)S(1)} %pad_clamp_fusion.1), kind=kCustom, calls=%fused_computation.1 | custom fusion | bytes 16777472 | tf_op jit(solution)/shard_map/gather | solution.py:54
  284.0 11.5 %convolution_bitcast_fusion = f32[64,128,512]{1,2,0:T(8,128)} fusion(bf16[64,128,512]{2,1,0:T(8,128)(2,1)} %gather_fusion.1, bf16[64,128,128]{2,1,0:T(8,128)(2,1)S(1)} %bitcast.47), kind=kOutput, calls=%fused_computation.17 | convolution fusion | flops 1073741824 | bytes 27262976 | tf_op jit(solution)/shard_map/sji,sjf->sif/dot_general | solution.py:53
  295.5 17.5 %copy.14 = f32[64,128,512]{2,1,0:T(8,128)} copy(f32[64,128,512]{1,2,0:T(8,128)} %convolution_bitcast_fusion) | data formatting | bytes 33554432 | tf_op jit(solution)/shard_map/sji,sjf->sif/dot_general | solution.py:53
  313.0 11.3 %broadcast_in_dim.19 = f32[128,128,512]{2,1,0:T(8,128)} broadcast(f32[]{:T(128)} %constant.5.clone.1), dimensions={} | broadcast | bytes 33554436 | tf_op jit(solution)/shard_map/broadcast_in_dim | solution.py:58
  324.3 36.3 %scatter_fusion.1 = f32[128,128,512]{2,1,0:T(8,128)} fusion(f32[128,128,512]{2,1,0:T(8,128)} %broadcast_in_dim.19, s32[64]{0:T(128)S(1)} %compare_select_fusion.3, f32[64,128,512]{2,1,0:T(8,128)} %copy.14), kind=kCustom, calls=%fused_computation.3 | custom fusion | flops 4194304 | bytes 50331904 | tf_op jit(solution)/shard_map/scatter-add | solution.py:59
  360.6 165.4 %reduce-scatter.5.cloned.1.call-done = f32[512,512]{1,0:T(8,128)} async-done(((f32[16384,512]{1,0:T(8,128)}), f32[512,512]{1,0:T(8,128)}) %reduce-scatter.5.cloned.1.call-update) | async-done | bytes 1048592 | tf_op jit(solution)/shard_map/reduce_scatter | solution.py:60
  530.2 148.8 %all-reduce.2.cloned.1.call-done = f32[512,512]{0,1:T(8,128)} async-done(((f32[512,512]{0,1:T(8,128)}), f32[512,512]{0,1:T(8,128)}) %all-reduce.2.cloned.1.call-update) | async-done | bytes 1048592 | tf_op jit(solution)/shard_map/psum | solution.py:73
  (65 shorter events, 43.4 us)
Async XLA Ops:
  7.2 1.1 copy-start
  7.2 80.0 %all-gather.3.cloned.1.call-start = ((), (), s32[]{:S(2)}) async-start(), calls=%async_computation.2 | async-start | bytes 17301504 | tf_op jit(solution)/shard_map/all_gather | solution.py:43
  10.5 232.9 %reduce-scatter.3.cloned.1.call-start = ((), (), s32[]{:S(2)}) async-start(), calls=%async_computation.3 | async-start | bytes 5242880 | tf_op jit(solution)/shard_map/reduce_scatter | solution.py:45
  196.9 46.5 %copy-start.3 = (bf16[512,512]{1,0:T(8,128)(2,1)S(1)}, bf16[512,512]{1,0:T(8,128)(2,1)}, u32[]{:S(2)}) copy-start(bf16[512,512]{1,0:T(8,128)(2,1)} %param.17) | copy-start | bytes 1572868
  196.9 46.5 %copy-start.5 = (f32[512]{0:T(512)S(1)}, f32[512]{0:T(512)}, u32[]{:S(2)}) copy-start(f32[512]{0:T(512)} %param.12) | copy-start | bytes 6148
  196.9 49.4 %copy-start.6 = (s32[64]{0:T(128)S(1)}, s32[64]{0:T(128)}, u32[]{:S(2)}) copy-start(s32[64]{0:T(128)} %param.14) | copy-start | bytes 772
  196.9 49.4 %copy-start.7 = (s32[64]{0:T(128)S(1)}, s32[64]{0:T(128)}, u32[]{:S(2)}) copy-start(s32[64]{0:T(128)} %param.15) | copy-start | bytes 772
  197.0 79.9 %all-gather.5.cloned.1.call-start = ((), (), s32[]{:S(2)}) async-start(), calls=%async_computation.4 | async-start | bytes 2621440 | tf_op jit(solution)/shard_map/all_gather | solution.py:51
  246.3 279.8 %reduce-scatter.5.cloned.1.call-start = ((), (), s32[]{:S(2)}) async-start(), calls=%async_computation.5 | async-start | bytes 34603008 | tf_op jit(solution)/shard_map/reduce_scatter | solution.py:60
  276.8 7.2 %copy-start.1 = (bf16[8,8,128,128]{3,2,1,0:T(8,128)(2,1)S(1)}, bf16[8,8,128,128]{3,2,1,0:T(8,128)(2,1)}, u32[]{:S(2)}) copy-start(bf16[8,8,128,128]{3,2,1,0:T(8,128)(2,1)} %get-tuple-element.130) | copy-start | bytes 6291460
  360.5 168.4 %copy-start.4 = (bf16[512,512]{1,0:T(8,128)(2,1)S(1)}, bf16[512,512]{1,0:T(8,128)(2,1)}, u32[]{:S(2)}) copy-start(bf16[512,512]{1,0:T(8,128)(2,1)} %param.11) | copy-start | bytes 1572868
  360.6 318.5 %all-reduce.2.cloned.1.call-start = ((), (), s32[]{:S(2)}) async-start(), calls=%async_computation.6 | async-start | bytes 2097152 | tf_op jit(solution)/shard_map/psum | solution.py:73
  526.1 2.9 copy-start.2
Sparse Core Ops, SparseCore 0:
  10.8 76.2 all-gather.2
  197.1 46.3 reduce-scatter.2
  246.4 30.3 all-gather.4
  360.7 165.3 reduce-scatter.4
  531.3 147.7 all-reduce.1
where the time goes:
time: 690 us; the launch traced here: 688 us
  waiting for transfers between devices  466 us (68%)
  local copies, waits for them, and re-layouts  101 us (15%)
  other arithmetic  74.4 us (11%)
  matrix products  31.8 us (5%)
  between operations  13.9 us (2%)
    reduce_scatter x1, waiting for transfers between devices, shards(): lax.psum_scatter(totals.reshape(nodes_dev * lax.axis_size('rows'), feat_w...  165 us
    psum x1, waiting for transfers between devices, shards(): grad_weight = lax.psum(local_weight, ('rows', 'rep'))  149 us
    all_gather x1, waiting for transfers between devices, shards(): panels = lax.all_gather(scaled, 'rows', axis=0, tiled=True)  75.1 us
    gather x8, local copies, waits for them, and re-layouts, add_group(): panel_blocks[group_cols]  58.8 us
    reduce_scatter x1, waiting for transfers between devices, shards(): lax.psum_scatter(slab_part, 'rep', scatter_dimension=0, tiled=True)  46.4 us
    scatter-add x1, other arithmetic, shards(): totals = totals.at[target].add(products, mode='drop')  36.3 us
    scatter-add x8, other arithmetic, add_group(): return (totals.at[group_rows].add(products), None)  34.5 us
    all_gather x1, waiting for transfers between devices, shards(): slab_grads = lax.all_gather(scaled_grad, 'rep', axis=0, tiled=True)  30.4 us
  transfers between devices with their start and end apart: 5, of which 5 were waited for; matrix products, arithmetic and copies ran while one was open for 0% of the time, Pallas kernels for 0%

commit v1 on v0

--- a/solution.py
+++ b/solution.py
@@ -40,7 +40,9 @@
     scaled = (jnp.dot(features, weight, preferred_element_type=jnp.float32) * row_scale).astype(
         jnp.bfloat16
     )
-    panels = lax.all_gather(scaled, "rows", axis=0, tiled=True)
+    panels = jnp.concatenate(
+        lax.all_to_all(jnp.stack([scaled] * lax.axis_size("rows")), "rows", 0, 0), axis=0
+    )
     slab_part = aggregate_slots(panels, tile_row, tile_col, tile_value, rep_count * block_count)
     aggregate = lax.psum_scatter(slab_part, "rep", scatter_dimension=0, tiled=True) * row_scale
     pre_act = aggregate + out_bias

time: 690 us -> 838 us (1.21)
  waiting for transfers between devices: 466 us -> 601 us
  starting transfers between devices: 0.21 us -> 9.77 us
    all_to_all x0 -> x1, waiting for transfers between devices: none -> 202 us  [shards(): lax.all_to_all(jnp.stack([scaled] * lax.axis_size('rows')), 'rows', 0, 0)]
    all_gather x1 -> x0, waiting for transfers between devices: 75.1 us -> none  [shards(): panels = lax.all_gather(scaled, 'rows', axis=0, tiled=True)]
    all_to_all x0 -> x1, starting transfers between devices: none -> 9.61 us  [shards(): lax.all_to_all(jnp.stack([scaled] * lax.axis_size('rows')), 'rows', 0, 0)]
    reduce_scatter x1, waiting for transfers between devices: 46.4 us -> 55 us  [shards(): lax.psum_scatter(slab_part, 'rep', scatter_dimension=0, tiled=True)]
where the time goes in v1:
time: 838 us; the launch traced here: 837 us
  waiting for transfers between devices  601 us (72%)
  local copies, waits for them, and re-layouts  106 us (13%)
  other arithmetic  74.2 us (9%)
  matrix products  32.1 us (4%)
  between operations  13.8 us (2%)
  starting transfers between devices  9.77 us (1%)
    all_to_all x1, waiting for transfers between devices, shards(): lax.all_to_all(jnp.stack([scaled] * lax.axis_size('rows')), 'rows', 0, 0)  202 us
    reduce_scatter x1, waiting for transfers between devices, shards(): lax.psum_scatter(totals.reshape(nodes_dev * lax.axis_size('rows'), feat_w...  165 us
    psum x1, waiting for transfers between devices, shards(): grad_weight = lax.psum(local_weight, ('rows', 'rep'))  148 us
    gather x8, local copies, waits for them, and re-layouts, add_group(): panel_blocks[group_cols]  58.9 us
    reduce_scatter x1, waiting for transfers between devices, shards(): lax.psum_scatter(slab_part, 'rep', scatter_dimension=0, tiled=True)  55 us
    scatter-add x1, other arithmetic, shards(): totals = totals.at[target].add(products, mode='drop')  36.1 us
    scatter-add x8, other arithmetic, add_group(): return (totals.at[group_rows].add(products), None)  34.4 us
    all_gather x1, waiting for transfers between devices, shards(): slab_grads = lax.all_gather(scaled_grad, 'rep', axis=0, tiled=True)  30.4 us
  transfers between devices with their start and end apart: 5, of which 5 were waited for; matrix products, arithmetic and copies ran while one was open for 0% of the time, Pallas kernels for 0%

profile of v1, /device:TPU:1, one launch (start us, length us, event | category | flops | bytes accessed | tf_op | source)
XLA Modules:
  0.0 836.7 jit_solution(15942530162691704051)
XLA Ops:
  9.7 5.9 stack.2
  15.7 9.6 %all-to-all-start = ((bf16[32,512,512]{2,1,0:T(8,128)(2,1)}), bf16[32,512,512]{2,1,0:T(8,128)(2,1)}, u32[]{:S(2)}, u32[]{:S(2)}) async-start(bf16[32,512,512]{2,1,0:T(8,128)(2,1)} %stack.2), calls=%async_computation | async-start | bytes 33554432 | tf_op jit(solution)/shard_map/all_to_all | solution.py:44
  25.5 201.9 %all-to-all-done = bf16[32,512,512]{2,1,0:T(8,128)(2,1)} async-done(((bf16[32,512,512]{2,1,0:T(8,128)(2,1)}), bf16[32,512,512]{2,1,0:T(8,128)(2,1)}, u32[]{:S(2)}, u32[]{:S(2)}) %all-to-all-start) | async-done | bytes 16777248 | tf_op jit(solution)/shard_map/all_to_all | solution.py:44
  229.8 107.2 %while.10 = (s32[]{:T(128)}, f32[16,128,512]{2,1,0:T(8,128)}, s32[8,8]{1,0:T(8,128)S(1)}, bf16[8,8,128,128]{3,2,1,0:T(8,128)(2,1)}, s32[8,8]{1,0:T(8,128)S(1)}, /*index=5*/bf16[128,128,512]{2,1,0:T(8,128)(2,1)}, s32[]{:T(128)}) while((s32[]{:T(128)}, f32[16,128,512]{2,1,0:T(8,128)}, s32[8,8]{1,0:T(8,128)S(1)}, ...), condition=%wide.region_2.3_spmd, body=%wide.region_0.2_spmd.sunk | while | flops 134743088 | bytes 11800893 | solution.py:29
  229.8 7.4 gather_fusion
  243.4 7.4 gather_fusion
  256.7 7.4 gather_fusion
  270.0 7.4 gather_fusion
  283.2 7.4 gather_fusion
  296.5 7.4 gather_fusion
  305.6 4.4 scatter_fusion
  310.0 7.4 gather_fusion
  319.1 4.4 scatter_fusion
  323.5 7.4 gather_fusion
  332.6 4.4 scatter_fusion
  337.1 55.0 %reduce-scatter.3.cloned.1.call-done = f32[512,512]{1,0:T(8,128)} async-done(((f32[2048,512]{1,0:T(8,128)}), f32[512,512]{1,0:T(8,128)}) %reduce-scatter.3.cloned.1.call-update) | async-done | bytes 1048592 | tf_op jit(solution)/shard_map/reduce_scatter | solution.py:47
  395.0 30.4 %all-gather.2.cloned.1.call-done = bf16[2048,512]{1,0:T(8,128)(2,1)} async-done(((bf16[512,512]{1,0:T(8,128)(2,1)}), bf16[2048,512]{1,0:T(8,128)(2,1)}) %all-gather.2.cloned.1.call-update) | async-done | bytes 2097168 | tf_op jit(solution)/shard_map/all_gather | solution.py:53
  425.5 7.2 gather_fusion.1
  432.7 11.5 %convolution_bitcast_fusion = f32[64,128,512]{1,2,0:T(8,128)} fusion(bf16[64,128,512]{2,1,0:T(8,128)(2,1)} %gather_fusion.1, bf16[64,128,128]{2,1,0:T(8,128)(2,1)S(1)} %bitcast.47), kind=kOutput, calls=%fused_computation.17 | convolution fusion | flops 1073741824 | bytes 27262976 | tf_op jit(solution)/shard_map/sji,sjf->sif/dot_general | solution.py:55
  444.2 17.4 %copy.14 = f32[64,128,512]{2,1,0:T(8,128)} copy(f32[64,128,512]{1,2,0:T(8,128)} %convolution_bitcast_fusion) | data formatting | bytes 33554432 | tf_op jit(solution)/shard_map/sji,sjf->sif/dot_general | solution.py:55
  461.6 11.3 %broadcast_in_dim.19 = f32[128,128,512]{2,1,0:T(8,128)} broadcast(f32[]{:T(128)} %constant.5.clone.1), dimensions={} | broadcast | bytes 33554436 | tf_op jit(solution)/shard_map/broadcast_in_dim | solution.py:60
  472.9 36.1 %scatter_fusion.1 = f32[128,128,512]{2,1,0:T(8,128)} fusion(f32[128,128,512]{2,1,0:T(8,128)} %broadcast_in_dim.19, s32[64]{0:T(128)S(1)} %compare_select_fusion.3, f32[64,128,512]{2,1,0:T(8,128)} %copy.14), kind=kCustom, calls=%fused_computation.3 | custom fusion | flops 4194304 | bytes 50331904 | tf_op jit(solution)/shard_map/scatter-add | solution.py:61
  509.1 165.5 %reduce-scatter.5.cloned.1.call-done = f32[512,512]{1,0:T(8,128)} async-done(((f32[16384,512]{1,0:T(8,128)}), f32[512,512]{1,0:T(8,128)}) %reduce-scatter.5.cloned.1.call-update) | async-done | bytes 1048592 | tf_op jit(solution)/shard_map/reduce_scatter | solution.py:62
  679.9 147.7 %all-reduce.2.cloned.1.call-done = f32[512,512]{0,1:T(8,128)} async-done(((f32[512,512]{0,1:T(8,128)}), f32[512,512]{0,1:T(8,128)}) %all-reduce.2.cloned.1.call-update) | async-done | bytes 1048592 | tf_op jit(solution)/shard_map/psum | solution.py:75
  (63 shorter events, 51.1 us)
Async XLA Ops:
  7.2 1.1 copy-start
  15.7 9.7 %copy-start.5 = (s32[64]{0:T(128)S(1)}, s32[64]{0:T(128)}, u32[]{:S(2)}) copy-start(s32[64]{0:T(128)} %param.14) | copy-start | bytes 772
  15.7 9.8 %copy-start.6 = (s32[64]{0:T(128)S(1)}, s32[64]{0:T(128)}, u32[]{:S(2)}) copy-start(s32[64]{0:T(128)} %param.15) | copy-start | bytes 772
  15.7 211.7 %all-to-all-start = ((bf16[32,512,512]{2,1,0:T(8,128)(2,1)}), bf16[32,512,512]{2,1,0:T(8,128)(2,1)}, u32[]{:S(2)}, u32[]{:S(2)}) async-start(bf16[32,512,512]{2,1,0:T(8,128)(2,1)} %stack.2), calls=%async_computation | async-start | bytes 33554432 | tf_op jit(solution)/shard_map/all_to_all | solution.py:44
  25.3 366.8 %reduce-scatter.3.cloned.1.call-start = ((), (), s32[]{:S(2)}) async-start(), calls=%async_computation.3 | async-start | bytes 5242880 | tf_op jit(solution)/shard_map/reduce_scatter | solution.py:47
  229.8 162.3 %copy-start.2 = (bf16[512,512]{1,0:T(8,128)(2,1)S(1)}, bf16[512,512]{1,0:T(8,128)(2,1)}, u32[]{:S(2)}) copy-start(bf16[512,512]{1,0:T(8,128)(2,1)} %param.17) | copy-start | bytes 1572868
  229.8 162.3 %copy-start.4 = (f32[512]{0:T(512)S(1)}, f32[512]{0:T(512)}, u32[]{:S(2)}) copy-start(f32[512]{0:T(512)} %param.12) | copy-start | bytes 6148
  337.1 88.4 %all-gather.2.cloned.1.call-start = ((), (), s32[]{:S(2)}) async-start(), calls=%async_computation.4 | async-start | bytes 2621440 | tf_op jit(solution)/shard_map/all_gather | solution.py:53
  394.9 279.7 %reduce-scatter.5.cloned.1.call-start = ((), (), s32[]{:S(2)}) async-start(), calls=%async_computation.5 | async-start | bytes 34603008 | tf_op jit(solution)/shard_map/reduce_scatter | solution.py:62
  425.5 7.2 copy-start.1
  509.0 168.3 %copy-start.3 = (bf16[512,512]{1,0:T(8,128)(2,1)S(1)}, bf16[512,512]{1,0:T(8,128)(2,1)}, u32[]{:S(2)}) copy-start(bf16[512,512]{1,0:T(8,128)(2,1)} %param.11) | copy-start | bytes 1572868
  509.1 318.6 %all-reduce.2.cloned.1.call-start = ((), (), s32[]{:S(2)}) async-start(), calls=%async_computation.6 | async-start | bytes 2097152 | tf_op jit(solution)/shard_map/psum | solution.py:75
Sparse Core Ops, SparseCore 0:
  337.2 54.8 reduce-scatter.2
  395.1 30.3 all-gather.1
  509.2 165.3 reduce-scatter.4
  679.8 147.7 all-reduce.1
